TPU v7x, 32 devices: a whole 2x2x4 slice. The times are simulated.
32 devices in a mesh: shot: 4 (over z), sub: 8 (over y, x, core).
Axes of the slice: x: 2, y: 2, z: 4, core: 2. Of those that a mesh axis runs over, the one named last changes fastest.
Arguments:
- electric: float32 [4, 3, 32, 32, 128], P('shot', None, 'sub'), may hold values from -6 to 6
- magnetic: float32 [4, 3, 32, 32, 128], P('shot', None, 'sub'), may hold values from -6 to 6
- polar: float32 [4, 3, 32, 32, 128], P('shot', None, 'sub'), may hold values from -4 to 4
- adj_electric: float32 [4, 3, 32, 32, 128], P('shot', None, 'sub'), may hold values from -6 to 6
- adj_magnetic: float32 [4, 3, 32, 32, 128], P('shot', None, 'sub'), may hold values from -6 to 6
- adj_polar: float32 [4, 3, 32, 32, 128], P('shot', None, 'sub'), may hold values from -4 to 4
- permittivity: float32 [32, 32, 128], P('sub'), may hold values from 3 to 25
- conductivity: float32 [32, 32, 128], P('sub'), may hold values from 0.02 to 2
- debye_class: int32 [32, 32, 128], P('sub'), may hold values from 0 to 7
- debye_rate: float32 [8], replicated, may hold values from 0.3 to 0.95
- debye_strength: float32 [8], replicated, may hold values from 0.3 to 3
- wavelet: float32 [6], replicated, may hold values from -4 to 4
- src_cell: int32 [4, 64], P('shot'), may hold values from 0 to 131071
- src_sign: int32 [4, 64], P('shot'), may hold values from 0 to 1
- rec_owner: int32 [4, 1024, 1], P('shot', 'sub'), may hold values from 0 to 7; in each aligned block of 128 rows (0 to 127, 128 to 255, ..., all dimensions but the last counted through in order) at most 16 rows name the same one
- rec_pos: int32 [4, 1024], P('shot', 'sub'), may hold values from 0 to 16383
- observed: float32 [4, 6, 1024], P('shot', None, 'sub'), may hold values from -6 to 6
Outputs:
- grad_eps: float32 [32, 32, 128], P('sub')
- grad_sigma: float32 [32, 32, 128], P('sub')
Inputs may be any that keep to these rules, and one draw needn't show every extreme that they name: Receiver r of a shot group lies in the x range of slab rec_owner; among the 128 receivers of each aligned block of the list at most 16 have the same owner.
All inputs are finite; a program needn't handle non-finite values.
Results may differ from a plain program's by a relative error of at most 0.0001.
Values sent between devices are 32-bit elements; how exact they have to be, the bound alone decides.
No kernel may reach another device: no remote copies, remote signals or barrier semaphores. Data moves between devices by JAX's collectives and lax.ppermute only.
A program may use at most 64 MiB of HBM per device.

v0:
```python
import jax
import jax.numpy as jnp
from jax import lax
from jax.sharding import PartitionSpec as P

CAP = 16


def from_behind(block, axis, distance):
    devices = range(lax.axis_size(axis))
    route = [(i - distance, i) for i in devices if i - distance in devices]
    return lax.ppermute(block, axis, route)


def diff_forward(u, axis):
    tail = lax.slice_in_dim(u, 1, u.shape[axis], axis=axis)
    edge = jnp.zeros_like(lax.slice_in_dim(u, 0, 1, axis=axis))
    return jnp.concatenate([tail, edge], axis) - u


def diff_backward(u, axis):
    head = lax.slice_in_dim(u, 0, u.shape[axis] - 1, axis=axis)
    edge = jnp.zeros_like(lax.slice_in_dim(u, 0, 1, axis=axis))
    return u - jnp.concatenate([edge, head], axis)


def forward_across(u, plane):
    return jnp.concatenate([u[1:], plane], 0) - u


def backward_across(u, plane):
    return u - jnp.concatenate([plane, u[:-1]], 0)


def advance(state, coefs, inject):
    e_field, h_field, p_field = state
    coef_a, coef_b, rate, strength = coefs
    east = from_behind(e_field[1:3, 0:1], "sub", -1)
    curl_e = jnp.stack(
        [
            diff_forward(e_field[2], 2) - diff_forward(e_field[1], 1),
            diff_forward(e_field[0], 1) - forward_across(e_field[2], east[1]),
            forward_across(e_field[1], east[0]) - diff_forward(e_field[0], 2),
        ]
    )
    h_new = h_field - 0.5 * curl_e
    west = from_behind(h_new[1:3, -1:], "sub", 1)
    curl_h = jnp.stack(
        [
            diff_backward(h_new[2], 2) - diff_backward(h_new[1], 1),
            diff_backward(h_new[0], 1) - backward_across(h_new[2], west[1]),
            backward_across(h_new[1], west[0]) - diff_backward(h_new[0], 2),
        ]
    )
    e_new = coef_a * e_field + coef_b * (curl_h - p_field)
    e_new = e_new.at[1].add(inject)
    p_new = rate * p_field + (1.0 - rate) * strength * e_new
    return (e_new, h_new, p_new)


def lookup(table, classes):
    picks = classes[None] == jnp.arange(table.shape[0], dtype=jnp.int32)[:, None, None, None]
    return jnp.sum(jnp.where(picks, table[:, None, None, None], 0.0), axis=0)


def per_device(
    electric,
    magnetic,
    polar,
    adj_electric,
    adj_magnetic,
    adj_polar,
    permittivity,
    conductivity,
    debye_class,
    debye_rate,
    debye_strength,
    wavelet,
    src_cell,
    src_sign,
    rec_owner,
    rec_pos,
    observed,
):
    width, depth, span = permittivity.shape
    steps = wavelet.shape[0]
    nsub = lax.axis_size("sub")
    nshot = lax.axis_size("shot")
    mine = lax.axis_index("sub")
    ratio = conductivity / (2.0 * permittivity)
    coefs = (
        (1.0 - ratio) / (1.0 + ratio),
        0.5 / (permittivity * (1.0 + ratio)),
        lookup(debye_rate, debye_class),
        lookup(debye_strength, debye_class),
    )
    full_x = width * nsub
    flat = src_cell[0]
    src_global = flat % full_x
    src_y = flat // full_x % span
    src_z = flat // (full_x * span)
    src_local = src_global - mine * width
    src_live = (src_local >= 0) & (src_local < width)
    src_x = jnp.clip(src_local, 0, width - 1)
    src_amp = jnp.where(src_live, (2 * src_sign[0] - 1).astype(jnp.float32), 0.0)
    owners = rec_owner[0, :, 0]
    cellpos = rec_pos[0]
    traces = observed[0]
    hits = (owners[:, None] == jnp.arange(nsub, dtype=jnp.int32)[None, :]).astype(jnp.int32)
    before = jnp.cumsum(hits, axis=0) - hits
    slots = jnp.sum(hits * before, axis=1)
    target = owners * CAP + slots
    send_trace = jnp.zeros((steps, nsub * CAP), jnp.float32).at[:, target].set(traces)
    send_pos = jnp.full((1, nsub * CAP), -1, jnp.int32).at[0, target].set(cellpos)
    got_trace, got_pos = (
        lax.all_to_all(send_trace, "sub", split_axis=1, concat_axis=1, tiled=True),
        lax.all_to_all(send_pos, "sub", split_axis=1, concat_axis=1, tiled=True),
    )
    positions = got_pos[0]
    live = positions >= 0
    positions = jnp.where(live, positions, 0)
    rec_x = positions % width
    rec_y = positions // width % span
    rec_z = positions // (width * span)
    state = (electric[0], magnetic[0], polar[0])
    history = [electric[0]]
    synth = []
    for step in range(steps):
        source = (
            jnp.zeros((width, depth, span), jnp.float32)
            .at[src_x, src_z, src_y]
            .add(src_amp * wavelet[step])
        )
        state = advance(state, coefs, source)
        history.append(state[0])
        synth.append(state[0][1][rec_x, rec_z, rec_y])
    resid = jnp.where(live[None], jnp.stack(synth) - got_trace, 0.0)
    state = (adj_electric[0], adj_magnetic[0], adj_polar[0])
    corr_eps = jnp.zeros((width, depth, span), jnp.float32)
    corr_sigma = jnp.zeros((width, depth, span), jnp.float32)
    for back in range(steps):
        later = steps - back
        source = (
            jnp.zeros((width, depth, span), jnp.float32)
            .at[rec_x, rec_z, rec_y]
            .add(resid[later - 1])
        )
        state = advance(state, coefs, source)
        adjoint = state[0]
        term_eps = jnp.sum(adjoint * (history[later] - history[later - 1]), axis=0)
        term_sigma = jnp.sum(adjoint * history[later], axis=0)
        corr_eps = corr_eps + term_eps
        corr_sigma = corr_sigma + term_sigma
    corr_eps, corr_sigma = lax.psum((corr_eps, corr_sigma), "shot")
    return (-(corr_eps / (steps * nshot)), -(corr_sigma / (steps * nshot)))


def solution(mesh):
    in_specs = (
        P("shot", None, "sub", None, None),
        P("shot", None, "sub", None, None),
        P("shot", None, "sub", None, None),
        P("shot", None, "sub", None, None),
        P("shot", None, "sub", None, None),
        P("shot", None, "sub", None, None),
        P("sub", None, None),
        P("sub", None, None),
        P("sub", None, None),
        P(),
        P(),
        P(),
        P("shot", None),
        P("shot", None),
        P("shot", "sub", None),
        P("shot", "sub"),
        P("shot", None, "sub"),
    )
    out_specs = (P("sub", None, None), P("sub", None, None))
    return jax.shard_map(
        per_device, mesh=mesh, in_specs=in_specs, out_specs=out_specs, check_vma=False
    )
```

profile of v0, /device:TPU:0, one launch (start us, length us, event | category | flops | bytes accessed | tf_op | source)
XLA Modules:
  0.0 288.4 jit_solution(6837316200168095393)
XLA Ops:
  13.6 7.1 %all-to-all-start = ((s32[1,8,16]{2,0,1:T(1,128)}), s32[1,8,16]{2,0,1:T(1,128)S(1)}, u32[]{:S(2)}, u32[]{:S(2)}) async-start(s32[1,8,16]{2,0,1:T(1,128)} %bitcast.28), calls=%async_computation | async-start | bytes 8192 | tf_op jit(solution)/shard_map/all_to_all | solution.py:117
  28.0 3.2 %broadcast_multiply_fusion.1 = (f32[64]{0:T(128)S(1)}, f32[64]{0:T(128)S(1)}, f32[64]{0:T(128)S(1)}, f32[64]{0:T(128)S(1)}, f32[64]{0:T(128)S(1)}) fusion(f32[64]{0:T(128)S(1)} %get-tuple-element.205, f32[]{:T(128)} %bitcast.150, f32[]{:T(128)} %bitcast.127, f32[]{:T(128)} %bitcast.104, f32[]{:T(128)} %bitcast.81, f32[]{:T(128)} %bitcast.57), kind=kLoop, calls=%fused_computation.540 | loop fusion | flops 320 | bytes 1556 | tf_op jit(solution)/shard_map/mul | solution.py:132
  31.2 4.5 %scatter_fusion = f32[4,32,128]{2,1,0:T(8,128)S(1)} fusion(f32[4,32,128]{2,1,0:T(8,128)S(1)} %broadcast.880.clone, s32[64]{0:T(128)S(1)} %fusion.152, f32[64]{0:T(128)S(1)} %get-tuple-element.440), kind=kCustom, calls=%fused_computation.7 | custom fusion | flops 64 | bytes 1536 | tf_op jit(solution)/shard_map/scatter-add | solution.py:132
  35.7 4.5 %scatter_fusion.1 = f32[4,32,128]{2,1,0:T(8,128)S(1)} fusion(f32[4,32,128]{2,1,0:T(8,128)S(1)} %broadcast.880.clone.1, s32[64]{0:T(128)S(1)} %fusion.152, f32[64]{0:T(128)S(1)} %get-tuple-element.439), kind=kCustom, calls=%fused_computation.8 | custom fusion | flops 64 | bytes 1536 | tf_op jit(solution)/shard_map/scatter-add | solution.py:132
  40.2 4.5 %scatter_fusion.2 = f32[4,32,128]{2,1,0:T(8,128)S(1)} fusion(f32[4,32,128]{2,1,0:T(8,128)S(1)} %broadcast.880.clone.2, s32[64]{0:T(128)S(1)} %fusion.152, f32[64]{0:T(128)S(1)} %get-tuple-element.438), kind=kCustom, calls=%fused_computation.9 | custom fusion | flops 64 | bytes 1536 | tf_op jit(solution)/shard_map/scatter-add | solution.py:132
  44.7 4.5 %scatter_fusion.3 = f32[4,32,128]{2,1,0:T(8,128)S(1)} fusion(f32[4,32,128]{2,1,0:T(8,128)S(1)} %broadcast.880.clone.3, s32[64]{0:T(128)S(1)} %fusion.152, f32[64]{0:T(128)S(1)} %get-tuple-element.437), kind=kCustom, calls=%fused_computation.10 | custom fusion | flops 64 | bytes 1536 | tf_op jit(solution)/shard_map/scatter-add | solution.py:132
  49.2 4.5 %scatter_fusion.4 = f32[4,32,128]{2,1,0:T(8,128)S(1)} fusion(f32[4,32,128]{2,1,0:T(8,128)S(1)} %broadcast.880.clone.4, s32[64]{0:T(128)S(1)} %fusion.152, f32[64]{0:T(128)S(1)} %get-tuple-element.436), kind=kCustom, calls=%fused_computation.11 | custom fusion | flops 64 | bytes 1536 | tf_op jit(solution)/shard_map/scatter-add | solution.py:132
  53.7 4.5 %scatter_fusion.5 = f32[4,32,128]{2,1,0:T(8,128)S(1)} fusion(f32[4,32,128]{2,1,0:T(8,128)S(1)} %broadcast.880.clone.6, s32[64]{0:T(128)S(1)} %fusion.152, f32[64]{0:T(128)S(1)} %get-tuple-element.204), kind=kCustom, calls=%fused_computation.12 | custom fusion | flops 64 | bytes 1536 | tf_op jit(solution)/shard_map/scatter-add | solution.py:132
  58.2 4.1 %all-to-all-start.1 = ((f32[6,8,16]{2,0,1:T(8,128)}), f32[6,8,16]{2,0,1:T(8,128)S(1)}, u32[]{:S(2)}, u32[]{:S(2)}) async-start(f32[6,8,16]{2,0,1:T(8,128)} %copy.45), calls=%async_computation.1 | async-start | bytes 65536 | tf_op jit(solution)/shard_map/all_to_all | solution.py:116
  64.3 2.9 %all-to-all-done.1 = f32[6,8,16]{2,0,1:T(8,128)S(1)} async-done(((f32[6,8,16]{2,0,1:T(8,128)}), f32[6,8,16]{2,0,1:T(8,128)S(1)}, u32[]{:S(2)}, u32[]{:S(2)}) %all-to-all-start.1) | async-done | bytes 3104 | tf_op jit(solution)/shard_map/all_to_all | solution.py:116
  68.9 1.6 collective-permute-start.3
  71.6 2.9 collective-permute-start.1
  75.6 1.3 collective-permute-start.4
  77.9 1.5 gather_fusion
  79.5 3.4 %collective-permute-start.5 = (f32[2,1,32,128]{3,2,1,0:T(8,128)S(1)}, f32[2,1,32,128]{3,2,1,0:T(8,128)S(1)}, u32[]{:S(2)}, u32[]{:S(2)}) collective-permute-start(f32[2,1,32,128]{3,2,1,0:T(8,128)S(1)} %slice.1953), channel_id=1, source_target_pairs={{0,1},{1,2},{2,3},{3,4},{4,5},{5,6},{6,7},{8,9},{9,10},{10,11},{11... | collective-permute-start | bytes 98312 | tf_op jit(solution)/shard_map/ppermute | solution.py:12
  84.0 1.3 collective-permute-start.6
  85.4 1.5 gather_fusion.1
  87.9 5.1 %collective-permute-start.7 = (f32[2,1,32,128]{3,2,1,0:T(8,128)S(1)}, f32[2,1,32,128]{3,2,1,0:T(8,128)S(1)}, u32[]{:S(2)}, u32[]{:S(2)}) collective-permute-start(f32[2,1,32,128]{3,2,1,0:T(8,128)S(1)} %slice.1977), channel_id=1, source_target_pairs={{0,1},{1,2},{2,3},{3,4},{4,5},{5,6},{6,7},{8,9},{9,10},{10,11},{11... | collective-permute-start | bytes 98312 | tf_op jit(solution)/shard_map/ppermute | solution.py:12
  94.2 1.5 collective-permute-start.8
  95.8 2.0 gather_fusion.2
  98.6 5.0 %collective-permute-start.9 = (f32[2,1,32,128]{3,2,1,0:T(8,128)S(1)}, f32[2,1,32,128]{3,2,1,0:T(8,128)S(1)}, u32[]{:S(2)}, u32[]{:S(2)}) collective-permute-start(f32[2,1,32,128]{3,2,1,0:T(8,128)S(1)} %slice.2001), channel_id=1, source_target_pairs={{0,1},{1,2},{2,3},{3,4},{4,5},{5,6},{6,7},{8,9},{9,10},{10,11},{11... | collective-permute-start | bytes 98312 | tf_op jit(solution)/shard_map/ppermute | solution.py:12
  108.1 2.0 gather_fusion.3
  112.1 3.6 %collective-permute-start.11 = (f32[2,1,32,128]{3,2,1,0:T(8,128)S(1)}, f32[2,1,32,128]{3,2,1,0:T(8,128)S(1)}, u32[]{:S(2)}, u32[]{:S(2)}) collective-permute-start(f32[2,1,32,128]{3,2,1,0:T(8,128)S(1)} %slice.2025), channel_id=1, source_target_pairs={{0,1},{1,2},{2,3},{3,4},{4,5},{5,6},{6,7},{8,9},{9,10},{10,11},{11... | collective-permute-start | bytes 98312 | tf_op jit(solution)/shard_map/ppermute | solution.py:12
  121.2 2.1 gather_fusion.4
  126.0 5.1 %collective-permute-start.13 = (f32[2,1,32,128]{3,2,1,0:T(8,128)S(1)}, f32[2,1,32,128]{3,2,1,0:T(8,128)S(1)}, u32[]{:S(2)}, u32[]{:S(2)}) collective-permute-start(f32[2,1,32,128]{3,2,1,0:T(8,128)S(1)} %slice.2049), channel_id=1, source_target_pairs={{0,1},{1,2},{2,3},{3,4},{4,5},{5,6},{6,7},{8,9},{9,10},{10,11},{11... | collective-permute-start | bytes 98312 | tf_op jit(solution)/shard_map/ppermute | solution.py:12
  133.2 1.5 gather_fusion.5
  135.9 8.3 %scatter_fusion.6 = f32[4,32,128]{2,1,0:T(8,128)S(1)} fusion(f32[4,32,128]{2,1,0:T(8,128)S(1)} %broadcast.880.clone.5, s32[128]{0:T(128)S(1)} %get-tuple-element.216, f32[128]{0:T(128)S(1)} %get-tuple-element.185), kind=kCustom, calls=%fused_computation.14 | custom fusion | flops 128 | bytes 3072 | tf_op jit(solution)/shard_map/scatter-add | solution.py:146
  144.3 1.3 collective-permute-start.14
  145.9 8.3 %scatter_fusion.7 = f32[4,32,128]{2,1,0:T(8,128)S(1)} fusion(f32[4,32,128]{2,1,0:T(8,128)S(1)} %broadcast.880.clone.7, s32[128]{0:T(128)S(1)} %get-tuple-element.216, f32[128]{0:T(128)S(1)} %get-tuple-element.184), kind=kCustom, calls=%fused_computation.15 | custom fusion | flops 128 | bytes 3072 | tf_op jit(solution)/shard_map/scatter-add | solution.py:146
  154.2 8.3 %scatter_fusion.8 = f32[4,32,128]{2,1,0:T(8,128)S(1)} fusion(f32[4,32,128]{2,1,0:T(8,128)S(1)} %broadcast.880.clone.8, s32[128]{0:T(128)S(1)} %get-tuple-element.216, f32[128]{0:T(128)S(1)} %get-tuple-element.183), kind=kCustom, calls=%fused_computation.16 | custom fusion | flops 128 | bytes 3072 | tf_op jit(solution)/shard_map/scatter-add | solution.py:146
  162.5 8.3 %scatter_fusion.9 = f32[4,32,128]{2,1,0:T(8,128)S(1)} fusion(f32[4,32,128]{2,1,0:T(8,128)S(1)} %broadcast.880.clone.9, s32[128]{0:T(128)S(1)} %get-tuple-element.216, f32[128]{0:T(128)S(1)} %get-tuple-element.182), kind=kCustom, calls=%fused_computation.17 | custom fusion | flops 128 | bytes 3072 | tf_op jit(solution)/shard_map/scatter-add | solution.py:146
  170.9 8.3 %scatter_fusion.10 = f32[4,32,128]{2,1,0:T(8,128)S(1)} fusion(f32[4,32,128]{2,1,0:T(8,128)S(1)} %broadcast.880.clone.10, s32[128]{0:T(128)S(1)} %get-tuple-element.216, f32[128]{0:T(128)S(1)} %get-tuple-element.181), kind=kCustom, calls=%fused_computation.18 | custom fusion | flops 128 | bytes 3072 | tf_op jit(solution)/shard_map/scatter-add | solution.py:146
  179.2 8.3 %scatter_fusion.11 = f32[4,32,128]{2,1,0:T(8,128)S(1)} fusion(f32[4,32,128]{2,1,0:T(8,128)S(1)} %broadcast.880.clone.11, s32[128]{0:T(128)S(1)} %get-tuple-element.216, f32[128]{0:T(128)S(1)} %get-tuple-element.180), kind=kCustom, calls=%fused_computation.19 | custom fusion | flops 128 | bytes 3072 | tf_op jit(solution)/shard_map/scatter-add | solution.py:146
  187.7 4.4 %collective-permute-start.15 = (f32[2,1,32,128]{3,2,1,0:T(8,128)S(1)}, f32[2,1,32,128]{3,2,1,0:T(8,128)S(1)}, u32[]{:S(2)}, u32[]{:S(2)}) collective-permute-start(f32[2,1,32,128]{3,2,1,0:T(8,128)S(1)} %slice.2074), channel_id=1, source_target_pairs={{0,1},{1,2},{2,3},{3,4},{4,5},{5,6},{6,7},{8,9},{9,10},{10,11},{11... | collective-permute-start | bytes 98312 | tf_op jit(solution)/shard_map/ppermute | solution.py:12
  193.3 1.3 collective-permute-start.16
  194.8 4.4 %collective-permute-done.16 = f32[2,1,32,128]{3,2,1,0:T(8,128)S(1)} collective-permute-done((f32[2,1,32,128]{3,2,1,0:T(8,128)S(1)}, f32[2,1,32,128]{3,2,1,0:T(8,128)S(1)}, u32[]{:S(2)}, u32[]{:S(2)}) %collective-permute-start.16) | collective-permute-done | bytes 32800 | tf_op jit(solution)/shard_map/ppermute | solution.py:12
  199.4 5.1 %collective-permute-start.17 = (f32[2,1,32,128]{3,2,1,0:T(8,128)S(1)}, f32[2,1,32,128]{3,2,1,0:T(8,128)S(1)}, u32[]{:S(2)}, u32[]{:S(2)}) collective-permute-start(f32[2,1,32,128]{3,2,1,0:T(8,128)S(1)} %slice.2099), channel_id=1, source_target_pairs={{0,1},{1,2},{2,3},{3,4},{4,5},{5,6},{6,7},{8,9},{9,10},{10,11},{11... | collective-permute-start | bytes 98312 | tf_op jit(solution)/shard_map/ppermute | solution.py:12
  205.7 1.3 collective-permute-start.18
  207.2 3.4 %collective-permute-done.18 = f32[2,1,32,128]{3,2,1,0:T(8,128)S(1)} collective-permute-done((f32[2,1,32,128]{3,2,1,0:T(8,128)S(1)}, f32[2,1,32,128]{3,2,1,0:T(8,128)S(1)}, u32[]{:S(2)}, u32[]{:S(2)}) %collective-permute-start.18) | collective-permute-done | bytes 32800 | tf_op jit(solution)/shard_map/ppermute | solution.py:12
  210.7 6.7 %collective-permute-start.19 = (f32[2,1,32,128]{3,2,1,0:T(8,128)S(1)}, f32[2,1,32,128]{3,2,1,0:T(8,128)S(1)}, u32[]{:S(2)}, u32[]{:S(2)}) collective-permute-start(f32[2,1,32,128]{3,2,1,0:T(8,128)S(1)} %slice.2124), channel_id=1, source_target_pairs={{0,1},{1,2},{2,3},{3,4},{4,5},{5,6},{6,7},{8,9},{9,10},{10,11},{11... | collective-permute-start | bytes 98312 | tf_op jit(solution)/shard_map/ppermute | solution.py:12
  218.7 1.3 collective-permute-start.20
  220.2 1.6 collective-permute-done.20
  222.0 5.7 %collective-permute-start.21 = (f32[2,1,32,128]{3,2,1,0:T(8,128)S(1)}, f32[2,1,32,128]{3,2,1,0:T(8,128)S(1)}, u32[]{:S(2)}, u32[]{:S(2)}) collective-permute-start(f32[2,1,32,128]{3,2,1,0:T(8,128)S(1)} %slice.2149), channel_id=1, source_target_pairs={{0,1},{1,2},{2,3},{3,4},{4,5},{5,6},{6,7},{8,9},{9,10},{10,11},{11... | collective-permute-start | bytes 98312 | tf_op jit(solution)/shard_map/ppermute | solution.py:12
  228.8 1.3 collective-permute-start.22
  230.3 1.6 collective-permute-done.22
  232.2 5.7 %collective-permute-start.23 = (f32[2,1,32,128]{3,2,1,0:T(8,128)S(1)}, f32[2,1,32,128]{3,2,1,0:T(8,128)S(1)}, u32[]{:S(2)}, u32[]{:S(2)}) collective-permute-start(f32[2,1,32,128]{3,2,1,0:T(8,128)S(1)} %slice.2174), channel_id=1, source_target_pairs={{0,1},{1,2},{2,3},{3,4},{4,5},{5,6},{6,7},{8,9},{9,10},{10,11},{11... | collective-permute-start | bytes 98312 | tf_op jit(solution)/shard_map/ppermute | solution.py:12
  240.7 38.6 %all-reduce.100.cloned.1.call-done = (f32[4,32,128]{2,1,0:T(8,128)}, f32[4,32,128]{2,1,0:T(8,128)}) async-done(((f32[4,32,128]{2,1,0:T(8,128)}, f32[4,32,128]{2,1,0:T(8,128)}), (f32[4,32,128]{2,1,0:T(8,128)}, f32[4,32,128]{2,1,0:T(8,128)})) %all-reduce.100.cloned.1.call-update) | async-done | bytes 131088 | tf_op jit(solution)/shard_map/psum | solution.py:154
  279.4 1.5 multiply_negate_fusion.1
  (362 shorter events, 51.7 us)
Async XLA Ops:
  7.2 4.2 %copy-start.31 = (s32[1,128,1]{1,2,0:T(1,128)S(1)}, s32[1,128,1]{1,2,0:T(1,128)}, u32[]{:S(2)}) copy-start(s32[1,128,1]{1,2,0:T(1,128)} %param.55) | copy-start | bytes 1540
  7.2 13.5 %copy-start.2 = (f32[1,3,4,32,128]{4,3,2,1,0:T(8,128)S(1)}, f32[1,3,4,32,128]{4,3,2,1,0:T(8,128)}, u32[]{:S(2)}) copy-start(f32[1,3,4,32,128]{4,3,2,1,0:T(8,128)} %param.41) | copy-start | bytes 589828
  8.0 59.9 %collective-permute-start.2 = (f32[2,1,32,128]{3,2,1,0:T(8,128)S(1)}, f32[2,1,32,128]{3,2,1,0:T(8,128)S(1)}, u32[]{:S(2)}, u32[]{:S(2)}) collective-permute-start(f32[2,1,32,128]{3,2,1,0:T(8,128)S(1)} %slice.1919), channel_id=1, source_target_pairs={{1,0},{2,1},{3,2},{4,3},{5,4},{6,5},{7,6},{9,8},{10,9},{11,10},{12... | collective-permute-start | bytes 98312 | tf_op jit(solution)/shard_map/ppermute | solution.py:12
  10.1 60.5 %collective-permute-start = (f32[2,1,32,128]{3,2,1,0:T(8,128)S(1)}, f32[2,1,32,128]{3,2,1,0:T(8,128)S(1)}, u32[]{:S(2)}, u32[]{:S(2)}) collective-permute-start(f32[2,1,32,128]{3,2,1,0:T(8,128)S(1)} %slice.1899), channel_id=1, source_target_pairs={{1,0},{2,1},{3,2},{4,3},{5,4},{6,5},{7,6},{9,8},{10,9},{11,10},{12... | collective-permute-start | bytes 98312 | tf_op jit(solution)/shard_map/ppermute | solution.py:12
  13.6 44.6 %all-to-all-start = ((s32[1,8,16]{2,0,1:T(1,128)}), s32[1,8,16]{2,0,1:T(1,128)S(1)}, u32[]{:S(2)}, u32[]{:S(2)}) async-start(s32[1,8,16]{2,0,1:T(1,128)} %bitcast.28), calls=%async_computation | async-start | bytes 8192 | tf_op jit(solution)/shard_map/all_to_all | solution.py:117
  20.7 0.9 copy-start.5
  24.0 1.7 copy-start.28
  25.7 2.0 copy-start.25
  58.2 8.9 %all-to-all-start.1 = ((f32[6,8,16]{2,0,1:T(8,128)}), f32[6,8,16]{2,0,1:T(8,128)S(1)}, u32[]{:S(2)}, u32[]{:S(2)}) async-start(f32[6,8,16]{2,0,1:T(8,128)} %copy.45), calls=%async_computation.1 | async-start | bytes 65536 | tf_op jit(solution)/shard_map/all_to_all | solution.py:116
  62.3 217.0 %all-reduce.100.cloned.1.call-start = ((), (), s32[]{:S(2)}) async-start(), calls=%async_computation.2 | async-start | bytes 262144 | tf_op jit(solution)/shard_map/psum | solution.py:154
  67.9 0.9 copy-start
  68.9 5.5 %collective-permute-start.3 = (f32[2,1,32,128]{3,2,1,0:T(8,128)S(1)}, f32[2,1,32,128]{3,2,1,0:T(8,128)S(1)}, u32[]{:S(2)}, u32[]{:S(2)}) collective-permute-start(f32[2,1,32,128]{3,2,1,0:T(8,128)S(1)} %slice.1929), channel_id=1, source_target_pairs={{0,1},{1,2},{2,3},{3,4},{4,5},{5,6},{6,7},{8,9},{9,10},{10,11},{11... | collective-permute-start | bytes 98312 | tf_op jit(solution)/shard_map/ppermute | solution.py:12
  70.6 0.9 copy-start.1
  71.6 5.2 %collective-permute-start.1 = (f32[2,1,32,128]{3,2,1,0:T(8,128)S(1)}, f32[2,1,32,128]{3,2,1,0:T(8,128)S(1)}, u32[]{:S(2)}, u32[]{:S(2)}) collective-permute-start(f32[2,1,32,128]{3,2,1,0:T(8,128)S(1)} %slice.1909), channel_id=1, source_target_pairs={{0,1},{1,2},{2,3},{3,4},{4,5},{5,6},{6,7},{8,9},{9,10},{10,11},{11... | collective-permute-start | bytes 98312 | tf_op jit(solution)/shard_map/ppermute | solution.py:12
  74.5 0.9 copy-start.3
  75.6 3.8 %collective-permute-start.4 = (f32[2,1,32,128]{3,2,1,0:T(8,128)S(1)}, f32[2,1,32,128]{3,2,1,0:T(8,128)S(1)}, u32[]{:S(2)}, u32[]{:S(2)}) collective-permute-start(f32[2,1,32,128]{3,2,1,0:T(8,128)S(1)} %slice.1942), channel_id=1, source_target_pairs={{1,0},{2,1},{3,2},{4,3},{5,4},{6,5},{7,6},{9,8},{10,9},{11,10},{12... | collective-permute-start | bytes 98312 | tf_op jit(solution)/shard_map/ppermute | solution.py:12
  79.5 4.2 %collective-permute-start.5 = (f32[2,1,32,128]{3,2,1,0:T(8,128)S(1)}, f32[2,1,32,128]{3,2,1,0:T(8,128)S(1)}, u32[]{:S(2)}, u32[]{:S(2)}) collective-permute-start(f32[2,1,32,128]{3,2,1,0:T(8,128)S(1)} %slice.1953), channel_id=1, source_target_pairs={{0,1},{1,2},{2,3},{3,4},{4,5},{5,6},{6,7},{8,9},{9,10},{10,11},{11... | collective-permute-start | bytes 98312 | tf_op jit(solution)/shard_map/ppermute | solution.py:12
  84.0 3.7 %collective-permute-start.6 = (f32[2,1,32,128]{3,2,1,0:T(8,128)S(1)}, f32[2,1,32,128]{3,2,1,0:T(8,128)S(1)}, u32[]{:S(2)}, u32[]{:S(2)}) collective-permute-start(f32[2,1,32,128]{3,2,1,0:T(8,128)S(1)} %slice.1966), channel_id=1, source_target_pairs={{1,0},{2,1},{3,2},{4,3},{5,4},{6,5},{7,6},{9,8},{10,9},{11,10},{12... | collective-permute-start | bytes 98312 | tf_op jit(solution)/shard_map/ppermute | solution.py:12
  87.9 6.0 %collective-permute-start.7 = (f32[2,1,32,128]{3,2,1,0:T(8,128)S(1)}, f32[2,1,32,128]{3,2,1,0:T(8,128)S(1)}, u32[]{:S(2)}, u32[]{:S(2)}) collective-permute-start(f32[2,1,32,128]{3,2,1,0:T(8,128)S(1)} %slice.1977), channel_id=1, source_target_pairs={{0,1},{1,2},{2,3},{3,4},{4,5},{5,6},{6,7},{8,9},{9,10},{10,11},{11... | collective-permute-start | bytes 98312 | tf_op jit(solution)/shard_map/ppermute | solution.py:12
  94.2 3.7 %collective-permute-start.8 = (f32[2,1,32,128]{3,2,1,0:T(8,128)S(1)}, f32[2,1,32,128]{3,2,1,0:T(8,128)S(1)}, u32[]{:S(2)}, u32[]{:S(2)}) collective-permute-start(f32[2,1,32,128]{3,2,1,0:T(8,128)S(1)} %slice.1990), channel_id=1, source_target_pairs={{1,0},{2,1},{3,2},{4,3},{5,4},{6,5},{7,6},{9,8},{10,9},{11,10},{12... | collective-permute-start | bytes 98312 | tf_op jit(solution)/shard_map/ppermute | solution.py:12
  98.6 5.9 %collective-permute-start.9 = (f32[2,1,32,128]{3,2,1,0:T(8,128)S(1)}, f32[2,1,32,128]{3,2,1,0:T(8,128)S(1)}, u32[]{:S(2)}, u32[]{:S(2)}) collective-permute-start(f32[2,1,32,128]{3,2,1,0:T(8,128)S(1)} %slice.2001), channel_id=1, source_target_pairs={{0,1},{1,2},{2,3},{3,4},{4,5},{5,6},{6,7},{8,9},{9,10},{10,11},{11... | collective-permute-start | bytes 98312 | tf_op jit(solution)/shard_map/ppermute | solution.py:12
  105.4 4.8 %collective-permute-start.10 = (f32[2,1,32,128]{3,2,1,0:T(8,128)S(1)}, f32[2,1,32,128]{3,2,1,0:T(8,128)S(1)}, u32[]{:S(2)}, u32[]{:S(2)}) collective-permute-start(f32[2,1,32,128]{3,2,1,0:T(8,128)S(1)} %slice.2014), channel_id=1, source_target_pairs={{1,0},{2,1},{3,2},{4,3},{5,4},{6,5},{7,6},{9,8},{10,9},{11,10},{12... | collective-permute-start | bytes 98312 | tf_op jit(solution)/shard_map/ppermute | solution.py:12
  111.1 0.9 copy-start.10
  112.1 4.4 %collective-permute-start.11 = (f32[2,1,32,128]{3,2,1,0:T(8,128)S(1)}, f32[2,1,32,128]{3,2,1,0:T(8,128)S(1)}, u32[]{:S(2)}, u32[]{:S(2)}) collective-permute-start(f32[2,1,32,128]{3,2,1,0:T(8,128)S(1)} %slice.2025), channel_id=1, source_target_pairs={{0,1},{1,2},{2,3},{3,4},{4,5},{5,6},{6,7},{8,9},{9,10},{10,11},{11... | collective-permute-start | bytes 98312 | tf_op jit(solution)/shard_map/ppermute | solution.py:12
  118.6 5.6 %collective-permute-start.12 = (f32[2,1,32,128]{3,2,1,0:T(8,128)}, f32[2,1,32,128]{3,2,1,0:T(8,128)}, u32[]{:S(2)}, u32[]{:S(2)}) collective-permute-start(f32[2,1,32,128]{3,2,1,0:T(8,128)} %slice.2038), channel_id=1, source_target_pairs={{1,0},{2,1},{3,2},{4,3},{5,4},{6,5},{7,6},{9,8},{10,9},{11,10},{12... | collective-permute-start | bytes 98312 | tf_op jit(solution)/shard_map/ppermute | solution.py:12
  121.2 2.1 copy-start.20
  123.3 1.6 copy-start.22
  123.3 1.6 copy-start.24
  123.4 1.5 copy-start.19
  126.0 5.9 %collective-permute-start.13 = (f32[2,1,32,128]{3,2,1,0:T(8,128)S(1)}, f32[2,1,32,128]{3,2,1,0:T(8,128)S(1)}, u32[]{:S(2)}, u32[]{:S(2)}) collective-permute-start(f32[2,1,32,128]{3,2,1,0:T(8,128)S(1)} %slice.2049), channel_id=1, source_target_pairs={{0,1},{1,2},{2,3},{3,4},{4,5},{5,6},{6,7},{8,9},{9,10},{10,11},{11... | collective-permute-start | bytes 98312 | tf_op jit(solution)/shard_map/ppermute | solution.py:12
  132.0 0.9 copy-start.4
  132.0 0.9 copy-start.14
  132.0 1.0 copy-start.15
  132.0 1.0 copy-start.16
  133.2 1.5 copy-start.32
  133.2 1.5 copy-start.33
  133.2 1.5 copy-start.34
  144.3 43.2 %collective-permute-start.14 = (f32[2,1,32,128]{3,2,1,0:T(8,128)S(1)}, f32[2,1,32,128]{3,2,1,0:T(8,128)S(1)}, u32[]{:S(2)}, u32[]{:S(2)}) collective-permute-start(f32[2,1,32,128]{3,2,1,0:T(8,128)S(1)} %slice.2063), channel_id=1, source_target_pairs={{1,0},{2,1},{3,2},{4,3},{5,4},{6,5},{7,6},{9,8},{10,9},{11,10},{12... | collective-permute-start | bytes 98312 | tf_op jit(solution)/shard_map/ppermute | solution.py:12
  187.7 5.3 %collective-permute-start.15 = (f32[2,1,32,128]{3,2,1,0:T(8,128)S(1)}, f32[2,1,32,128]{3,2,1,0:T(8,128)S(1)}, u32[]{:S(2)}, u32[]{:S(2)}) collective-permute-start(f32[2,1,32,128]{3,2,1,0:T(8,128)S(1)} %slice.2074), channel_id=1, source_target_pairs={{0,1},{1,2},{2,3},{3,4},{4,5},{5,6},{6,7},{8,9},{9,10},{10,11},{11... | collective-permute-start | bytes 98312 | tf_op jit(solution)/shard_map/ppermute | solution.py:12
  193.3 5.9 %collective-permute-start.16 = (f32[2,1,32,128]{3,2,1,0:T(8,128)S(1)}, f32[2,1,32,128]{3,2,1,0:T(8,128)S(1)}, u32[]{:S(2)}, u32[]{:S(2)}) collective-permute-start(f32[2,1,32,128]{3,2,1,0:T(8,128)S(1)} %slice.2088), channel_id=1, source_target_pairs={{1,0},{2,1},{3,2},{4,3},{5,4},{6,5},{7,6},{9,8},{10,9},{11,10},{12... | collective-permute-start | bytes 98312 | tf_op jit(solution)/shard_map/ppermute | solution.py:12
  199.4 6.0 %collective-permute-start.17 = (f32[2,1,32,128]{3,2,1,0:T(8,128)S(1)}, f32[2,1,32,128]{3,2,1,0:T(8,128)S(1)}, u32[]{:S(2)}, u32[]{:S(2)}) collective-permute-start(f32[2,1,32,128]{3,2,1,0:T(8,128)S(1)} %slice.2099), channel_id=1, source_target_pairs={{0,1},{1,2},{2,3},{3,4},{4,5},{5,6},{6,7},{8,9},{9,10},{10,11},{11... | collective-permute-start | bytes 98312 | tf_op jit(solution)/shard_map/ppermute | solution.py:12
  205.7 4.9 %collective-permute-start.18 = (f32[2,1,32,128]{3,2,1,0:T(8,128)S(1)}, f32[2,1,32,128]{3,2,1,0:T(8,128)S(1)}, u32[]{:S(2)}, u32[]{:S(2)}) collective-permute-start(f32[2,1,32,128]{3,2,1,0:T(8,128)S(1)} %slice.2113), channel_id=1, source_target_pairs={{1,0},{2,1},{3,2},{4,3},{5,4},{6,5},{7,6},{9,8},{10,9},{11,10},{12... | collective-permute-start | bytes 98312 | tf_op jit(solution)/shard_map/ppermute | solution.py:12
  210.7 7.6 %collective-permute-start.19 = (f32[2,1,32,128]{3,2,1,0:T(8,128)S(1)}, f32[2,1,32,128]{3,2,1,0:T(8,128)S(1)}, u32[]{:S(2)}, u32[]{:S(2)}) collective-permute-start(f32[2,1,32,128]{3,2,1,0:T(8,128)S(1)} %slice.2124), channel_id=1, source_target_pairs={{0,1},{1,2},{2,3},{3,4},{4,5},{5,6},{6,7},{8,9},{9,10},{10,11},{11... | collective-permute-start | bytes 98312 | tf_op jit(solution)/shard_map/ppermute | solution.py:12
  218.7 3.1 %collective-permute-start.20 = (f32[2,1,32,128]{3,2,1,0:T(8,128)S(1)}, f32[2,1,32,128]{3,2,1,0:T(8,128)S(1)}, u32[]{:S(2)}, u32[]{:S(2)}) collective-permute-start(f32[2,1,32,128]{3,2,1,0:T(8,128)S(1)} %slice.2138), channel_id=1, source_target_pairs={{1,0},{2,1},{3,2},{4,3},{5,4},{6,5},{7,6},{9,8},{10,9},{11,10},{12... | collective-permute-start | bytes 98312 | tf_op jit(solution)/shard_map/ppermute | solution.py:12
  222.0 6.5 %collective-permute-start.21 = (f32[2,1,32,128]{3,2,1,0:T(8,128)S(1)}, f32[2,1,32,128]{3,2,1,0:T(8,128)S(1)}, u32[]{:S(2)}, u32[]{:S(2)}) collective-permute-start(f32[2,1,32,128]{3,2,1,0:T(8,128)S(1)} %slice.2149), channel_id=1, source_target_pairs={{0,1},{1,2},{2,3},{3,4},{4,5},{5,6},{6,7},{8,9},{9,10},{10,11},{11... | collective-permute-start | bytes 98312 | tf_op jit(solution)/shard_map/ppermute | solution.py:12
  228.8 3.1 %collective-permute-start.22 = (f32[2,1,32,128]{3,2,1,0:T(8,128)S(1)}, f32[2,1,32,128]{3,2,1,0:T(8,128)S(1)}, u32[]{:S(2)}, u32[]{:S(2)}) collective-permute-start(f32[2,1,32,128]{3,2,1,0:T(8,128)S(1)} %slice.2163), channel_id=1, source_target_pairs={{1,0},{2,1},{3,2},{4,3},{5,4},{6,5},{7,6},{9,8},{10,9},{11,10},{12... | collective-permute-start | bytes 98312 | tf_op jit(solution)/shard_map/ppermute | solution.py:12
  232.2 6.5 %collective-permute-start.23 = (f32[2,1,32,128]{3,2,1,0:T(8,128)S(1)}, f32[2,1,32,128]{3,2,1,0:T(8,128)S(1)}, u32[]{:S(2)}, u32[]{:S(2)}) collective-permute-start(f32[2,1,32,128]{3,2,1,0:T(8,128)S(1)} %slice.2174), channel_id=1, source_target_pairs={{0,1},{1,2},{2,3},{3,4},{4,5},{5,6},{6,7},{8,9},{9,10},{10,11},{11... | collective-permute-start | bytes 98312 | tf_op jit(solution)/shard_map/ppermute | solution.py:12
  279.4 1.5 copy-start.26
  (19 other events, 14.5 us)
Sparse Core Ops, SparseCore 0:
  240.8 38.4 all-reduce.99
where the time goes:
time: 290 us; the launch traced here: 288 us
  other arithmetic  91.1 us (31%)
  starting transfers between devices  81.2 us (28%)
  waiting for transfers between devices  62.3 us (21%)
  local copies, waits for them, and re-layouts  37.8 us (13%)
  between operations  16 us (6%)
    ppermute x24, starting transfers between devices, from_behind(): return lax.ppermute(block, axis, route)  70 us
    scatter-add x6, other arithmetic, per_device(): source = jnp.zeros((width, depth, span), jnp.float32).at[rec_x, rec_z, re...  49.9 us
    psum x1, waiting for transfers between devices, per_device(): corr_eps, corr_sigma = lax.psum((corr_eps, corr_sigma), 'shot')  38.6 us
    scatter-add x6, other arithmetic, per_device(): source = jnp.zeros((width, depth, span), jnp.float32).at[src_x, src_z, sr...  26.9 us
    ppermute x24, waiting for transfers between devices, from_behind(): return lax.ppermute(block, axis, route)  20.8 us
    gather x6, local copies, waits for them, and re-layouts, per_device(): synth.append(state[0][1][rec_x, rec_z, rec_y])  10.6 us
    unnamed x80, local copies, waits for them, and re-layouts  10.5 us
    all_to_all x1, starting transfers between devices, per_device(): lax.all_to_all(send_pos, 'sub', split_axis=1, concat_axis=1, tiled=True)  7.05 us
  transfers between devices with their start and end apart: 27, of which 18 were waited for; matrix products, arithmetic and copies ran while one was open for 33% of the time, Pallas kernels for 0%

commit v1 on v0

--- a/solution.py
+++ b/solution.py
@@ -4,6 +4,13 @@
 from jax.sharding import PartitionSpec as P
 
 CAP = 16
+
+
+def stacked_exchange(x, axis, split, join):
+    size = lax.axis_size(axis)
+    shards = jnp.stack(jnp.split(x, size, axis=split), axis=0)
+    shards = lax.all_to_all(shards, axis, split_axis=0, concat_axis=0)
+    return jnp.concatenate(shards, axis=join)
 
 
 def from_behind(block, axis, distance):
@@ -113,7 +120,7 @@
     send_trace = jnp.zeros((steps, nsub * CAP), jnp.float32).at[:, target].set(traces)
     send_pos = jnp.full((1, nsub * CAP), -1, jnp.int32).at[0, target].set(cellpos)
     got_trace, got_pos = (
-        lax.all_to_all(send_trace, "sub", split_axis=1, concat_axis=1, tiled=True),
+        stacked_exchange(send_trace, "sub", 1, 1),
         lax.all_to_all(send_pos, "sub", split_axis=1, concat_axis=1, tiled=True),
     )
     positions = got_pos[0]

time: 290 us -> 294 us (1.014)
  local copies, waits for them, and re-layouts: 37.8 us -> 42.4 us
    unnamed x80 -> x87, local copies, waits for them, and re-layouts: 10.5 us -> 14.6 us
  transfers between devices with their start and end apart: 27 -> 27, of which waited for: 18 -> 18; matrix products, arithmetic and copies ran while one was open for 33% -> 34% of each run, Pallas kernels for 0% -> 0%
where the time goes in v1:
time: 294 us; the launch traced here: 293 us
  other arithmetic  91.1 us (31%)
  starting transfers between devices  81.1 us (28%)
  waiting for transfers between devices  62.3 us (21%)
  local copies, waits for them, and re-layouts  42.4 us (14%)
  between operations  16 us (5%)
    ppermute x24, starting transfers between devices, from_behind(): return lax.ppermute(block, axis, route)  69.9 us
    scatter-add x6, other arithmetic, per_device(): source = jnp.zeros((width, depth, span), jnp.float32).at[rec_x, rec_z, re...  49.9 us
    psum x1, waiting for transfers between devices, per_device(): corr_eps, corr_sigma = lax.psum((corr_eps, corr_sigma), 'shot')  38.6 us
    scatter-add x6, other arithmetic, per_device(): source = jnp.zeros((width, depth, span), jnp.float32).at[src_x, src_z, sr...  26.9 us
    ppermute x24, waiting for transfers between devices, from_behind(): return lax.ppermute(block, axis, route)  20.8 us
    unnamed x87, local copies, waits for them, and re-layouts  14.6 us
    gather x6, local copies, waits for them, and re-layouts, per_device(): synth.append(state[0][1][rec_x, rec_z, rec_y])  10.6 us
    all_to_all x1, starting transfers between devices, per_device(): lax.all_to_all(send_pos, 'sub', split_axis=1, concat_axis=1, tiled=True)  7.05 us
  transfers between devices with their start and end apart: 27, of which 18 were waited for; matrix products, arithmetic and copies ran while one was open for 34% of the time, Pallas kernels for 0%

profile of v1, /device:TPU:0, one launch (start us, length us, event | category | flops | bytes accessed | tf_op | source)
XLA Modules:
  0.0 292.9 jit_solution(10729337079450704631)
XLA Ops:
  13.6 7.1 %all-to-all-start = ((s32[1,8,16]{2,0,1:T(1,128)}), s32[1,8,16]{2,0,1:T(1,128)S(1)}, u32[]{:S(2)}, u32[]{:S(2)}) async-start(s32[1,8,16]{2,0,1:T(1,128)} %bitcast.28), calls=%async_computation | async-start | bytes 8192 | tf_op jit(solution)/shard_map/all_to_all | solution.py:124
  28.5 3.1 %broadcast_multiply_fusion.1 = (f32[64]{0:T(128)S(1)}, f32[64]{0:T(128)S(1)}, f32[64]{0:T(128)S(1)}, f32[64]{0:T(128)S(1)}, f32[64]{0:T(128)S(1)}) fusion(f32[64]{0:T(128)S(1)} %get-tuple-element.205, f32[]{:T(128)} %bitcast.150, f32[]{:T(128)} %bitcast.127, f32[]{:T(128)} %bitcast.104, f32[]{:T(128)} %bitcast.81, f32[]{:T(128)} %bitcast.57), kind=kLoop, calls=%fused_computation.548 | loop fusion | flops 320 | bytes 1556 | tf_op jit(solution)/shard_map/mul | solution.py:139
  31.6 4.5 %scatter_fusion = f32[4,32,128]{2,1,0:T(8,128)S(1)} fusion(f32[4,32,128]{2,1,0:T(8,128)S(1)} %broadcast.880.clone, s32[64]{0:T(128)S(1)} %fusion.152, f32[64]{0:T(128)S(1)} %get-tuple-element.448), kind=kCustom, calls=%fused_computation.7 | custom fusion | flops 64 | bytes 1536 | tf_op jit(solution)/shard_map/scatter-add | solution.py:139
  36.1 4.5 %scatter_fusion.1 = f32[4,32,128]{2,1,0:T(8,128)S(1)} fusion(f32[4,32,128]{2,1,0:T(8,128)S(1)} %broadcast.880.clone.1, s32[64]{0:T(128)S(1)} %fusion.152, f32[64]{0:T(128)S(1)} %get-tuple-element.447), kind=kCustom, calls=%fused_computation.8 | custom fusion | flops 64 | bytes 1536 | tf_op jit(solution)/shard_map/scatter-add | solution.py:139
  40.6 4.5 %scatter_fusion.2 = f32[4,32,128]{2,1,0:T(8,128)S(1)} fusion(f32[4,32,128]{2,1,0:T(8,128)S(1)} %broadcast.880.clone.2, s32[64]{0:T(128)S(1)} %fusion.152, f32[64]{0:T(128)S(1)} %get-tuple-element.446), kind=kCustom, calls=%fused_computation.9 | custom fusion | flops 64 | bytes 1536 | tf_op jit(solution)/shard_map/scatter-add | solution.py:139
  49.3 4.5 %scatter_fusion.3 = f32[4,32,128]{2,1,0:T(8,128)S(1)} fusion(f32[4,32,128]{2,1,0:T(8,128)S(1)} %broadcast.880.clone.3, s32[64]{0:T(128)S(1)} %fusion.152, f32[64]{0:T(128)S(1)} %get-tuple-element.445), kind=kCustom, calls=%fused_computation.10 | custom fusion | flops 64 | bytes 1536 | tf_op jit(solution)/shard_map/scatter-add | solution.py:139
  53.8 4.5 %scatter_fusion.4 = f32[4,32,128]{2,1,0:T(8,128)S(1)} fusion(f32[4,32,128]{2,1,0:T(8,128)S(1)} %broadcast.880.clone.4, s32[64]{0:T(128)S(1)} %fusion.152, f32[64]{0:T(128)S(1)} %get-tuple-element.444), kind=kCustom, calls=%fused_computation.11 | custom fusion | flops 64 | bytes 1536 | tf_op jit(solution)/shard_map/scatter-add | solution.py:139
  58.3 4.5 %scatter_fusion.5 = f32[4,32,128]{2,1,0:T(8,128)S(1)} fusion(f32[4,32,128]{2,1,0:T(8,128)S(1)} %broadcast.880.clone.6, s32[64]{0:T(128)S(1)} %fusion.152, f32[64]{0:T(128)S(1)} %get-tuple-element.204), kind=kCustom, calls=%fused_computation.12 | custom fusion | flops 64 | bytes 1536 | tf_op jit(solution)/shard_map/scatter-add | solution.py:139
  62.8 4.1 %all-to-all-start.1 = ((f32[8,6,16]{2,1,0:T(8,128)}), f32[8,6,16]{2,1,0:T(8,128)S(1)}, u32[]{:S(2)}, u32[]{:S(2)}) async-start(f32[8,6,16]{2,1,0:T(8,128)} %constant_dynamic-update-slice_fusion), calls=%async_computation.1 | async-start | bytes 65536 | tf_op jit(solution)/shard_map/all_to_all | solution.py:12
  68.9 2.8 all-to-all-done.1
  73.5 1.6 collective-permute-start.3
  76.2 2.9 collective-permute-start.1
  80.1 1.3 collective-permute-start.4
  82.4 1.5 gather_fusion
  84.1 3.4 %collective-permute-start.5 = (f32[2,1,32,128]{3,2,1,0:T(8,128)S(1)}, f32[2,1,32,128]{3,2,1,0:T(8,128)S(1)}, u32[]{:S(2)}, u32[]{:S(2)}) collective-permute-start(f32[2,1,32,128]{3,2,1,0:T(8,128)S(1)} %slice.1953), channel_id=1, source_target_pairs={{0,1},{1,2},{2,3},{3,4},{4,5},{5,6},{6,7},{8,9},{9,10},{10,11},{11... | collective-permute-start | bytes 98312 | tf_op jit(solution)/shard_map/ppermute | solution.py:19
  88.6 1.3 collective-permute-start.6
  90.0 1.5 gather_fusion.1
  92.4 5.1 %collective-permute-start.7 = (f32[2,1,32,128]{3,2,1,0:T(8,128)S(1)}, f32[2,1,32,128]{3,2,1,0:T(8,128)S(1)}, u32[]{:S(2)}, u32[]{:S(2)}) collective-permute-start(f32[2,1,32,128]{3,2,1,0:T(8,128)S(1)} %slice.1977), channel_id=1, source_target_pairs={{0,1},{1,2},{2,3},{3,4},{4,5},{5,6},{6,7},{8,9},{9,10},{10,11},{11... | collective-permute-start | bytes 98312 | tf_op jit(solution)/shard_map/ppermute | solution.py:19
  98.7 1.5 collective-permute-start.8
  100.3 2.0 gather_fusion.2
  103.2 5.0 %collective-permute-start.9 = (f32[2,1,32,128]{3,2,1,0:T(8,128)S(1)}, f32[2,1,32,128]{3,2,1,0:T(8,128)S(1)}, u32[]{:S(2)}, u32[]{:S(2)}) collective-permute-start(f32[2,1,32,128]{3,2,1,0:T(8,128)S(1)} %slice.2001), channel_id=1, source_target_pairs={{0,1},{1,2},{2,3},{3,4},{4,5},{5,6},{6,7},{8,9},{9,10},{10,11},{11... | collective-permute-start | bytes 98312 | tf_op jit(solution)/shard_map/ppermute | solution.py:19
  112.6 2.1 gather_fusion.3
  116.6 3.6 %collective-permute-start.11 = (f32[2,1,32,128]{3,2,1,0:T(8,128)S(1)}, f32[2,1,32,128]{3,2,1,0:T(8,128)S(1)}, u32[]{:S(2)}, u32[]{:S(2)}) collective-permute-start(f32[2,1,32,128]{3,2,1,0:T(8,128)S(1)} %slice.2025), channel_id=1, source_target_pairs={{0,1},{1,2},{2,3},{3,4},{4,5},{5,6},{6,7},{8,9},{9,10},{10,11},{11... | collective-permute-start | bytes 98312 | tf_op jit(solution)/shard_map/ppermute | solution.py:19
  125.8 2.0 gather_fusion.4
  130.6 5.1 %collective-permute-start.13 = (f32[2,1,32,128]{3,2,1,0:T(8,128)S(1)}, f32[2,1,32,128]{3,2,1,0:T(8,128)S(1)}, u32[]{:S(2)}, u32[]{:S(2)}) collective-permute-start(f32[2,1,32,128]{3,2,1,0:T(8,128)S(1)} %slice.2049), channel_id=1, source_target_pairs={{0,1},{1,2},{2,3},{3,4},{4,5},{5,6},{6,7},{8,9},{9,10},{10,11},{11... | collective-permute-start | bytes 98312 | tf_op jit(solution)/shard_map/ppermute | solution.py:19
  137.8 1.5 gather_fusion.5
  140.5 8.3 %scatter_fusion.6 = f32[4,32,128]{2,1,0:T(8,128)S(1)} fusion(f32[4,32,128]{2,1,0:T(8,128)S(1)} %broadcast.880.clone.5, s32[128]{0:T(128)S(1)} %get-tuple-element.216, f32[128]{0:T(128)S(1)} %get-tuple-element.185), kind=kCustom, calls=%fused_computation.14 | custom fusion | flops 128 | bytes 3072 | tf_op jit(solution)/shard_map/scatter-add | solution.py:153
  148.9 1.3 collective-permute-start.14
  150.4 8.3 %scatter_fusion.7 = f32[4,32,128]{2,1,0:T(8,128)S(1)} fusion(f32[4,32,128]{2,1,0:T(8,128)S(1)} %broadcast.880.clone.7, s32[128]{0:T(128)S(1)} %get-tuple-element.216, f32[128]{0:T(128)S(1)} %get-tuple-element.184), kind=kCustom, calls=%fused_computation.15 | custom fusion | flops 128 | bytes 3072 | tf_op jit(solution)/shard_map/scatter-add | solution.py:153
  158.8 8.3 %scatter_fusion.8 = f32[4,32,128]{2,1,0:T(8,128)S(1)} fusion(f32[4,32,128]{2,1,0:T(8,128)S(1)} %broadcast.880.clone.8, s32[128]{0:T(128)S(1)} %get-tuple-element.216, f32[128]{0:T(128)S(1)} %get-tuple-element.183), kind=kCustom, calls=%fused_computation.16 | custom fusion | flops 128 | bytes 3072 | tf_op jit(solution)/shard_map/scatter-add | solution.py:153
  167.1 8.3 %scatter_fusion.9 = f32[4,32,128]{2,1,0:T(8,128)S(1)} fusion(f32[4,32,128]{2,1,0:T(8,128)S(1)} %broadcast.880.clone.9, s32[128]{0:T(128)S(1)} %get-tuple-element.216, f32[128]{0:T(128)S(1)} %get-tuple-element.182), kind=kCustom, calls=%fused_computation.17 | custom fusion | flops 128 | bytes 3072 | tf_op jit(solution)/shard_map/scatter-add | solution.py:153
  175.5 8.3 %scatter_fusion.10 = f32[4,32,128]{2,1,0:T(8,128)S(1)} fusion(f32[4,32,128]{2,1,0:T(8,128)S(1)} %broadcast.880.clone.10, s32[128]{0:T(128)S(1)} %get-tuple-element.216, f32[128]{0:T(128)S(1)} %get-tuple-element.181), kind=kCustom, calls=%fused_computation.18 | custom fusion | flops 128 | bytes 3072 | tf_op jit(solution)/shard_map/scatter-add | solution.py:153
  183.8 8.3 %scatter_fusion.11 = f32[4,32,128]{2,1,0:T(8,128)S(1)} fusion(f32[4,32,128]{2,1,0:T(8,128)S(1)} %broadcast.880.clone.11, s32[128]{0:T(128)S(1)} %get-tuple-element.216, f32[128]{0:T(128)S(1)} %get-tuple-element.180), kind=kCustom, calls=%fused_computation.19 | custom fusion | flops 128 | bytes 3072 | tf_op jit(solution)/shard_map/scatter-add | solution.py:153
  192.3 4.4 %collective-permute-start.15 = (f32[2,1,32,128]{3,2,1,0:T(8,128)S(1)}, f32[2,1,32,128]{3,2,1,0:T(8,128)S(1)}, u32[]{:S(2)}, u32[]{:S(2)}) collective-permute-start(f32[2,1,32,128]{3,2,1,0:T(8,128)S(1)} %slice.2074), channel_id=1, source_target_pairs={{0,1},{1,2},{2,3},{3,4},{4,5},{5,6},{6,7},{8,9},{9,10},{10,11},{11... | collective-permute-start | bytes 98312 | tf_op jit(solution)/shard_map/ppermute | solution.py:19
  197.8 1.3 collective-permute-start.16
  199.3 4.5 %collective-permute-done.16 = f32[2,1,32,128]{3,2,1,0:T(8,128)S(1)} collective-permute-done((f32[2,1,32,128]{3,2,1,0:T(8,128)S(1)}, f32[2,1,32,128]{3,2,1,0:T(8,128)S(1)}, u32[]{:S(2)}, u32[]{:S(2)}) %collective-permute-start.16) | collective-permute-done | bytes 32800 | tf_op jit(solution)/shard_map/ppermute | solution.py:19
  204.0 5.1 %collective-permute-start.17 = (f32[2,1,32,128]{3,2,1,0:T(8,128)S(1)}, f32[2,1,32,128]{3,2,1,0:T(8,128)S(1)}, u32[]{:S(2)}, u32[]{:S(2)}) collective-permute-start(f32[2,1,32,128]{3,2,1,0:T(8,128)S(1)} %slice.2099), channel_id=1, source_target_pairs={{0,1},{1,2},{2,3},{3,4},{4,5},{5,6},{6,7},{8,9},{9,10},{10,11},{11... | collective-permute-start | bytes 98312 | tf_op jit(solution)/shard_map/ppermute | solution.py:19
  210.2 1.3 collective-permute-start.18
  211.8 3.3 %collective-permute-done.18 = f32[2,1,32,128]{3,2,1,0:T(8,128)S(1)} collective-permute-done((f32[2,1,32,128]{3,2,1,0:T(8,128)S(1)}, f32[2,1,32,128]{3,2,1,0:T(8,128)S(1)}, u32[]{:S(2)}, u32[]{:S(2)}) %collective-permute-start.18) | collective-permute-done | bytes 32800 | tf_op jit(solution)/shard_map/ppermute | solution.py:19
  215.3 6.7 %collective-permute-start.19 = (f32[2,1,32,128]{3,2,1,0:T(8,128)S(1)}, f32[2,1,32,128]{3,2,1,0:T(8,128)S(1)}, u32[]{:S(2)}, u32[]{:S(2)}) collective-permute-start(f32[2,1,32,128]{3,2,1,0:T(8,128)S(1)} %slice.2124), channel_id=1, source_target_pairs={{0,1},{1,2},{2,3},{3,4},{4,5},{5,6},{6,7},{8,9},{9,10},{10,11},{11... | collective-permute-start | bytes 98312 | tf_op jit(solution)/shard_map/ppermute | solution.py:19
  223.2 1.3 collective-permute-start.20
  224.7 1.6 collective-permute-done.20
  226.5 5.7 %collective-permute-start.21 = (f32[2,1,32,128]{3,2,1,0:T(8,128)S(1)}, f32[2,1,32,128]{3,2,1,0:T(8,128)S(1)}, u32[]{:S(2)}, u32[]{:S(2)}) collective-permute-start(f32[2,1,32,128]{3,2,1,0:T(8,128)S(1)} %slice.2149), channel_id=1, source_target_pairs={{0,1},{1,2},{2,3},{3,4},{4,5},{5,6},{6,7},{8,9},{9,10},{10,11},{11... | collective-permute-start | bytes 98312 | tf_op jit(solution)/shard_map/ppermute | solution.py:19
  233.4 1.3 collective-permute-start.22
  234.9 1.6 collective-permute-done.22
  236.7 5.7 %collective-permute-start.23 = (f32[2,1,32,128]{3,2,1,0:T(8,128)S(1)}, f32[2,1,32,128]{3,2,1,0:T(8,128)S(1)}, u32[]{:S(2)}, u32[]{:S(2)}) collective-permute-start(f32[2,1,32,128]{3,2,1,0:T(8,128)S(1)} %slice.2174), channel_id=1, source_target_pairs={{0,1},{1,2},{2,3},{3,4},{4,5},{5,6},{6,7},{8,9},{9,10},{10,11},{11... | collective-permute-start | bytes 98312 | tf_op jit(solution)/shard_map/ppermute | solution.py:19
  245.2 38.6 %all-reduce.100.cloned.1.call-done = (f32[4,32,128]{2,1,0:T(8,128)}, f32[4,32,128]{2,1,0:T(8,128)}) async-done(((f32[4,32,128]{2,1,0:T(8,128)}, f32[4,32,128]{2,1,0:T(8,128)}), (f32[4,32,128]{2,1,0:T(8,128)}, f32[4,32,128]{2,1,0:T(8,128)})) %all-reduce.100.cloned.1.call-update) | async-done | bytes 131088 | tf_op jit(solution)/shard_map/psum | solution.py:161
  283.9 1.5 multiply_negate_fusion.1
  (378 shorter events, 56.5 us)
Async XLA Ops:
  7.2 4.2 %copy-start.31 = (s32[1,128,1]{1,2,0:T(1,128)S(1)}, s32[1,128,1]{1,2,0:T(1,128)}, u32[]{:S(2)}) copy-start(s32[1,128,1]{1,2,0:T(1,128)} %param.55) | copy-start | bytes 1540
  7.2 13.5 %copy-start.2 = (f32[1,3,4,32,128]{4,3,2,1,0:T(8,128)S(1)}, f32[1,3,4,32,128]{4,3,2,1,0:T(8,128)}, u32[]{:S(2)}) copy-start(f32[1,3,4,32,128]{4,3,2,1,0:T(8,128)} %param.41) | copy-start | bytes 589828
  8.0 64.5 %collective-permute-start.2 = (f32[2,1,32,128]{3,2,1,0:T(8,128)S(1)}, f32[2,1,32,128]{3,2,1,0:T(8,128)S(1)}, u32[]{:S(2)}, u32[]{:S(2)}) collective-permute-start(f32[2,1,32,128]{3,2,1,0:T(8,128)S(1)} %slice.1919), channel_id=1, source_target_pairs={{1,0},{2,1},{3,2},{4,3},{5,4},{6,5},{7,6},{9,8},{10,9},{11,10},{12... | collective-permute-start | bytes 98312 | tf_op jit(solution)/shard_map/ppermute | solution.py:19
  10.1 65.1 %collective-permute-start = (f32[2,1,32,128]{3,2,1,0:T(8,128)S(1)}, f32[2,1,32,128]{3,2,1,0:T(8,128)S(1)}, u32[]{:S(2)}, u32[]{:S(2)}) collective-permute-start(f32[2,1,32,128]{3,2,1,0:T(8,128)S(1)} %slice.1899), channel_id=1, source_target_pairs={{1,0},{2,1},{3,2},{4,3},{5,4},{6,5},{7,6},{9,8},{10,9},{11,10},{12... | collective-permute-start | bytes 98312 | tf_op jit(solution)/shard_map/ppermute | solution.py:19
  13.6 49.2 %all-to-all-start = ((s32[1,8,16]{2,0,1:T(1,128)}), s32[1,8,16]{2,0,1:T(1,128)S(1)}, u32[]{:S(2)}, u32[]{:S(2)}) async-start(s32[1,8,16]{2,0,1:T(1,128)} %bitcast.28), calls=%async_computation | async-start | bytes 8192 | tf_op jit(solution)/shard_map/all_to_all | solution.py:124
  20.7 0.9 copy-start.5
  24.9 1.3 copy-start.28
  24.9 1.3 copy-start.27
  26.2 2.1 copy-start.25
  62.8 8.9 %all-to-all-start.1 = ((f32[8,6,16]{2,1,0:T(8,128)}), f32[8,6,16]{2,1,0:T(8,128)S(1)}, u32[]{:S(2)}, u32[]{:S(2)}) async-start(f32[8,6,16]{2,1,0:T(8,128)} %constant_dynamic-update-slice_fusion), calls=%async_computation.1 | async-start | bytes 65536 | tf_op jit(solution)/shard_map/all_to_all | solution.py:12
  66.9 217.0 %all-reduce.100.cloned.1.call-start = ((), (), s32[]{:S(2)}) async-start(), calls=%async_computation.2 | async-start | bytes 262144 | tf_op jit(solution)/shard_map/psum | solution.py:161
  72.5 0.9 copy-start
  73.5 5.5 %collective-permute-start.3 = (f32[2,1,32,128]{3,2,1,0:T(8,128)S(1)}, f32[2,1,32,128]{3,2,1,0:T(8,128)S(1)}, u32[]{:S(2)}, u32[]{:S(2)}) collective-permute-start(f32[2,1,32,128]{3,2,1,0:T(8,128)S(1)} %slice.1929), channel_id=1, source_target_pairs={{0,1},{1,2},{2,3},{3,4},{4,5},{5,6},{6,7},{8,9},{9,10},{10,11},{11... | collective-permute-start | bytes 98312 | tf_op jit(solution)/shard_map/ppermute | solution.py:19
  75.2 0.9 copy-start.1
  76.2 5.2 %collective-permute-start.1 = (f32[2,1,32,128]{3,2,1,0:T(8,128)S(1)}, f32[2,1,32,128]{3,2,1,0:T(8,128)S(1)}, u32[]{:S(2)}, u32[]{:S(2)}) collective-permute-start(f32[2,1,32,128]{3,2,1,0:T(8,128)S(1)} %slice.1909), channel_id=1, source_target_pairs={{0,1},{1,2},{2,3},{3,4},{4,5},{5,6},{6,7},{8,9},{9,10},{10,11},{11... | collective-permute-start | bytes 98312 | tf_op jit(solution)/shard_map/ppermute | solution.py:19
  79.1 0.9 copy-start.3
  80.1 3.8 %collective-permute-start.4 = (f32[2,1,32,128]{3,2,1,0:T(8,128)S(1)}, f32[2,1,32,128]{3,2,1,0:T(8,128)S(1)}, u32[]{:S(2)}, u32[]{:S(2)}) collective-permute-start(f32[2,1,32,128]{3,2,1,0:T(8,128)S(1)} %slice.1942), channel_id=1, source_target_pairs={{1,0},{2,1},{3,2},{4,3},{5,4},{6,5},{7,6},{9,8},{10,9},{11,10},{12... | collective-permute-start | bytes 98312 | tf_op jit(solution)/shard_map/ppermute | solution.py:19
  84.1 4.2 %collective-permute-start.5 = (f32[2,1,32,128]{3,2,1,0:T(8,128)S(1)}, f32[2,1,32,128]{3,2,1,0:T(8,128)S(1)}, u32[]{:S(2)}, u32[]{:S(2)}) collective-permute-start(f32[2,1,32,128]{3,2,1,0:T(8,128)S(1)} %slice.1953), channel_id=1, source_target_pairs={{0,1},{1,2},{2,3},{3,4},{4,5},{5,6},{6,7},{8,9},{9,10},{10,11},{11... | collective-permute-start | bytes 98312 | tf_op jit(solution)/shard_map/ppermute | solution.py:19
  88.6 3.7 %collective-permute-start.6 = (f32[2,1,32,128]{3,2,1,0:T(8,128)S(1)}, f32[2,1,32,128]{3,2,1,0:T(8,128)S(1)}, u32[]{:S(2)}, u32[]{:S(2)}) collective-permute-start(f32[2,1,32,128]{3,2,1,0:T(8,128)S(1)} %slice.1966), channel_id=1, source_target_pairs={{1,0},{2,1},{3,2},{4,3},{5,4},{6,5},{7,6},{9,8},{10,9},{11,10},{12... | collective-permute-start | bytes 98312 | tf_op jit(solution)/shard_map/ppermute | solution.py:19
  92.4 6.0 %collective-permute-start.7 = (f32[2,1,32,128]{3,2,1,0:T(8,128)S(1)}, f32[2,1,32,128]{3,2,1,0:T(8,128)S(1)}, u32[]{:S(2)}, u32[]{:S(2)}) collective-permute-start(f32[2,1,32,128]{3,2,1,0:T(8,128)S(1)} %slice.1977), channel_id=1, source_target_pairs={{0,1},{1,2},{2,3},{3,4},{4,5},{5,6},{6,7},{8,9},{9,10},{10,11},{11... | collective-permute-start | bytes 98312 | tf_op jit(solution)/shard_map/ppermute | solution.py:19
  98.7 3.7 %collective-permute-start.8 = (f32[2,1,32,128]{3,2,1,0:T(8,128)S(1)}, f32[2,1,32,128]{3,2,1,0:T(8,128)S(1)}, u32[]{:S(2)}, u32[]{:S(2)}) collective-permute-start(f32[2,1,32,128]{3,2,1,0:T(8,128)S(1)} %slice.1990), channel_id=1, source_target_pairs={{1,0},{2,1},{3,2},{4,3},{5,4},{6,5},{7,6},{9,8},{10,9},{11,10},{12... | collective-permute-start | bytes 98312 | tf_op jit(solution)/shard_map/ppermute | solution.py:19
  103.2 5.9 %collective-permute-start.9 = (f32[2,1,32,128]{3,2,1,0:T(8,128)S(1)}, f32[2,1,32,128]{3,2,1,0:T(8,128)S(1)}, u32[]{:S(2)}, u32[]{:S(2)}) collective-permute-start(f32[2,1,32,128]{3,2,1,0:T(8,128)S(1)} %slice.2001), channel_id=1, source_target_pairs={{0,1},{1,2},{2,3},{3,4},{4,5},{5,6},{6,7},{8,9},{9,10},{10,11},{11... | collective-permute-start | bytes 98312 | tf_op jit(solution)/shard_map/ppermute | solution.py:19
  110.0 4.8 %collective-permute-start.10 = (f32[2,1,32,128]{3,2,1,0:T(8,128)S(1)}, f32[2,1,32,128]{3,2,1,0:T(8,128)S(1)}, u32[]{:S(2)}, u32[]{:S(2)}) collective-permute-start(f32[2,1,32,128]{3,2,1,0:T(8,128)S(1)} %slice.2014), channel_id=1, source_target_pairs={{1,0},{2,1},{3,2},{4,3},{5,4},{6,5},{7,6},{9,8},{10,9},{11,10},{12... | collective-permute-start | bytes 98312 | tf_op jit(solution)/shard_map/ppermute | solution.py:19
  116.6 4.4 %collective-permute-start.11 = (f32[2,1,32,128]{3,2,1,0:T(8,128)S(1)}, f32[2,1,32,128]{3,2,1,0:T(8,128)S(1)}, u32[]{:S(2)}, u32[]{:S(2)}) collective-permute-start(f32[2,1,32,128]{3,2,1,0:T(8,128)S(1)} %slice.2025), channel_id=1, source_target_pairs={{0,1},{1,2},{2,3},{3,4},{4,5},{5,6},{6,7},{8,9},{9,10},{10,11},{11... | collective-permute-start | bytes 98312 | tf_op jit(solution)/shard_map/ppermute | solution.py:19
  123.2 5.6 %collective-permute-start.12 = (f32[2,1,32,128]{3,2,1,0:T(8,128)}, f32[2,1,32,128]{3,2,1,0:T(8,128)}, u32[]{:S(2)}, u32[]{:S(2)}) collective-permute-start(f32[2,1,32,128]{3,2,1,0:T(8,128)} %slice.2038), channel_id=1, source_target_pairs={{1,0},{2,1},{3,2},{4,3},{5,4},{6,5},{7,6},{9,8},{10,9},{11,10},{12... | collective-permute-start | bytes 98312 | tf_op jit(solution)/shard_map/ppermute | solution.py:19
  125.8 2.0 copy-start.20
  127.8 1.7 copy-start.22
  127.8 1.7 copy-start.24
  127.9 1.6 copy-start.19
  130.6 5.9 %collective-permute-start.13 = (f32[2,1,32,128]{3,2,1,0:T(8,128)S(1)}, f32[2,1,32,128]{3,2,1,0:T(8,128)S(1)}, u32[]{:S(2)}, u32[]{:S(2)}) collective-permute-start(f32[2,1,32,128]{3,2,1,0:T(8,128)S(1)} %slice.2049), channel_id=1, source_target_pairs={{0,1},{1,2},{2,3},{3,4},{4,5},{5,6},{6,7},{8,9},{9,10},{10,11},{11... | collective-permute-start | bytes 98312 | tf_op jit(solution)/shard_map/ppermute | solution.py:19
  136.5 0.9 copy-start.4
  136.5 0.9 copy-start.14
  136.5 1.0 copy-start.15
  136.6 1.0 copy-start.16
  137.7 1.5 copy-start.32
  137.8 1.5 copy-start.33
  137.8 1.5 copy-start.34
  148.9 43.2 %collective-permute-start.14 = (f32[2,1,32,128]{3,2,1,0:T(8,128)S(1)}, f32[2,1,32,128]{3,2,1,0:T(8,128)S(1)}, u32[]{:S(2)}, u32[]{:S(2)}) collective-permute-start(f32[2,1,32,128]{3,2,1,0:T(8,128)S(1)} %slice.2063), channel_id=1, source_target_pairs={{1,0},{2,1},{3,2},{4,3},{5,4},{6,5},{7,6},{9,8},{10,9},{11,10},{12... | collective-permute-start | bytes 98312 | tf_op jit(solution)/shard_map/ppermute | solution.py:19
  192.3 5.2 %collective-permute-start.15 = (f32[2,1,32,128]{3,2,1,0:T(8,128)S(1)}, f32[2,1,32,128]{3,2,1,0:T(8,128)S(1)}, u32[]{:S(2)}, u32[]{:S(2)}) collective-permute-start(f32[2,1,32,128]{3,2,1,0:T(8,128)S(1)} %slice.2074), channel_id=1, source_target_pairs={{0,1},{1,2},{2,3},{3,4},{4,5},{5,6},{6,7},{8,9},{9,10},{10,11},{11... | collective-permute-start | bytes 98312 | tf_op jit(solution)/shard_map/ppermute | solution.py:19
  197.8 6.0 %collective-permute-start.16 = (f32[2,1,32,128]{3,2,1,0:T(8,128)S(1)}, f32[2,1,32,128]{3,2,1,0:T(8,128)S(1)}, u32[]{:S(2)}, u32[]{:S(2)}) collective-permute-start(f32[2,1,32,128]{3,2,1,0:T(8,128)S(1)} %slice.2088), channel_id=1, source_target_pairs={{1,0},{2,1},{3,2},{4,3},{5,4},{6,5},{7,6},{9,8},{10,9},{11,10},{12... | collective-permute-start | bytes 98312 | tf_op jit(solution)/shard_map/ppermute | solution.py:19
  204.0 6.0 %collective-permute-start.17 = (f32[2,1,32,128]{3,2,1,0:T(8,128)S(1)}, f32[2,1,32,128]{3,2,1,0:T(8,128)S(1)}, u32[]{:S(2)}, u32[]{:S(2)}) collective-permute-start(f32[2,1,32,128]{3,2,1,0:T(8,128)S(1)} %slice.2099), channel_id=1, source_target_pairs={{0,1},{1,2},{2,3},{3,4},{4,5},{5,6},{6,7},{8,9},{9,10},{10,11},{11... | collective-permute-start | bytes 98312 | tf_op jit(solution)/shard_map/ppermute | solution.py:19
  210.2 4.8 %collective-permute-start.18 = (f32[2,1,32,128]{3,2,1,0:T(8,128)S(1)}, f32[2,1,32,128]{3,2,1,0:T(8,128)S(1)}, u32[]{:S(2)}, u32[]{:S(2)}) collective-permute-start(f32[2,1,32,128]{3,2,1,0:T(8,128)S(1)} %slice.2113), channel_id=1, source_target_pairs={{1,0},{2,1},{3,2},{4,3},{5,4},{6,5},{7,6},{9,8},{10,9},{11,10},{12... | collective-permute-start | bytes 98312 | tf_op jit(solution)/shard_map/ppermute | solution.py:19
  215.3 7.6 %collective-permute-start.19 = (f32[2,1,32,128]{3,2,1,0:T(8,128)S(1)}, f32[2,1,32,128]{3,2,1,0:T(8,128)S(1)}, u32[]{:S(2)}, u32[]{:S(2)}) collective-permute-start(f32[2,1,32,128]{3,2,1,0:T(8,128)S(1)} %slice.2124), channel_id=1, source_target_pairs={{0,1},{1,2},{2,3},{3,4},{4,5},{5,6},{6,7},{8,9},{9,10},{10,11},{11... | collective-permute-start | bytes 98312 | tf_op jit(solution)/shard_map/ppermute | solution.py:19
  223.2 3.1 %collective-permute-start.20 = (f32[2,1,32,128]{3,2,1,0:T(8,128)S(1)}, f32[2,1,32,128]{3,2,1,0:T(8,128)S(1)}, u32[]{:S(2)}, u32[]{:S(2)}) collective-permute-start(f32[2,1,32,128]{3,2,1,0:T(8,128)S(1)} %slice.2138), channel_id=1, source_target_pairs={{1,0},{2,1},{3,2},{4,3},{5,4},{6,5},{7,6},{9,8},{10,9},{11,10},{12... | collective-permute-start | bytes 98312 | tf_op jit(solution)/shard_map/ppermute | solution.py:19
  226.5 6.5 %collective-permute-start.21 = (f32[2,1,32,128]{3,2,1,0:T(8,128)S(1)}, f32[2,1,32,128]{3,2,1,0:T(8,128)S(1)}, u32[]{:S(2)}, u32[]{:S(2)}) collective-permute-start(f32[2,1,32,128]{3,2,1,0:T(8,128)S(1)} %slice.2149), channel_id=1, source_target_pairs={{0,1},{1,2},{2,3},{3,4},{4,5},{5,6},{6,7},{8,9},{9,10},{10,11},{11... | collective-permute-start | bytes 98312 | tf_op jit(solution)/shard_map/ppermute | solution.py:19
  233.4 3.1 %collective-permute-start.22 = (f32[2,1,32,128]{3,2,1,0:T(8,128)S(1)}, f32[2,1,32,128]{3,2,1,0:T(8,128)S(1)}, u32[]{:S(2)}, u32[]{:S(2)}) collective-permute-start(f32[2,1,32,128]{3,2,1,0:T(8,128)S(1)} %slice.2163), channel_id=1, source_target_pairs={{1,0},{2,1},{3,2},{4,3},{5,4},{6,5},{7,6},{9,8},{10,9},{11,10},{12... | collective-permute-start | bytes 98312 | tf_op jit(solution)/shard_map/ppermute | solution.py:19
  236.7 6.5 %collective-permute-start.23 = (f32[2,1,32,128]{3,2,1,0:T(8,128)S(1)}, f32[2,1,32,128]{3,2,1,0:T(8,128)S(1)}, u32[]{:S(2)}, u32[]{:S(2)}) collective-permute-start(f32[2,1,32,128]{3,2,1,0:T(8,128)S(1)} %slice.2174), channel_id=1, source_target_pairs={{0,1},{1,2},{2,3},{3,4},{4,5},{5,6},{6,7},{8,9},{9,10},{10,11},{11... | collective-permute-start | bytes 98312 | tf_op jit(solution)/shard_map/ppermute | solution.py:19
  283.9 1.5 copy-start.26
  (19 other events, 14.6 us)
Sparse Core Ops, SparseCore 0:
  245.4 38.4 all-reduce.99
